TPU v7x, 32 devices: a whole 2x2x4 slice. The times are simulated.
32 devices in a mesh: tok: 4 (over y, x), hid: 8 (over z, core).
Axes of the slice: x: 2, y: 2, z: 4, core: 2. Of those that a mesh axis runs over, the one named last changes fastest.
Arguments:
- tokens: bfloat16 [6144, 6144], P('tok', 'hid'), may hold values from -6 to 6
- cotangent: bfloat16 [6144, 6144], P('tok', 'hid'), may hold values from -6 to 6
- expert_choice: int32 [6144, 2], P('tok'), may hold values from 0 to 7, as said below
- router: bfloat16 [8, 6144], replicated, may hold values from -0.078125 to 0.078125
- gate_up: bfloat16 [6144, 2, 8192], P('tok', None, 'hid'), may hold values from -0.109375 to 0.109375
- w_down: bfloat16 [6144, 8192], P('tok', 'hid'), may hold values from -0.0625 to 0.0625
Outputs:
- grad_tokens: bfloat16 [6144, 6144], P('tok', 'hid')
- d_combine: float32 [6144, 2], P('tok')
- d_gate_up: float32 [6144, 2, 8192], P('tok', None, 'hid')
- d_down: float32 [6144, 8192], P('tok', 'hid')
Inputs may be any that keep to these rules, and one draw needn't show every extreme that they name: `expert_choice`: each row names 2 different experts. In every aligned block of 1536 rows at most 432 rows name expert 0 and at least half of 432 do; some block has exactly 432.
All inputs are finite; a program needn't handle non-finite values.
Results may differ from a plain program's by a relative error of at most 0.017.
Values may be sent and summed in bfloat16 or wider, within the bound.
A program may use at most 128 MiB of HBM per device.

v0:
```python
import jax
import jax.numpy as jnp
from jax import lax
from jax.sharding import PartitionSpec as P

CAP = 432


def silu_pair(pre):
    sigma = jax.nn.sigmoid(pre)
    return (pre * sigma, sigma * (1.0 + pre * (1.0 - sigma)))


def contract_rows(left, right):
    return lax.dot_general(
        left, right, (((0,), (0,)), ((), ())), preferred_element_type=jnp.float32
    )


def contract_cols(left, right):
    return lax.dot_general(
        left, right, (((1,), (1,)), ((), ())), preferred_element_type=jnp.float32
    )


def local_grads(joined, raw, slot_gate):
    width = raw.shape[1]
    gate_pre = joined[:, :width]
    up_pre = joined[:, width:]
    active, slope = silu_pair(gate_pre)
    product = active * up_pre
    scale = slot_gate[:, None]
    scaled = (scale * product).astype(jnp.bfloat16)
    score_part = jnp.sum(product * raw, axis=1)
    upstream = scale * raw
    grads_mid = jnp.concatenate(
        [
            (upstream * up_pre * slope).astype(jnp.bfloat16),
            (upstream * active).astype(jnp.bfloat16),
        ],
        axis=1,
    )
    return (grads_mid, scaled, score_part)


def local(tokens, cotangent, expert_choice, router, gate_up, w_down):
    local_cols = tokens.shape[1]
    weight_rows = w_down.shape[0]
    hidden_local = w_down.shape[1]
    first = expert_choice[:, 0]
    second = expert_choice[:, 1]
    in_first = first == 0
    in_second = second == 0
    routed = jnp.logical_or(in_first, in_second)
    flags = routed.astype(jnp.int32)
    slot_rank = jnp.cumsum(flags) - flags
    slot_ids = jnp.arange(CAP, dtype=jnp.int32)
    placed = jnp.logical_and(routed[None, :], slot_rank[None, :] == slot_ids[:, None])
    stacked = jnp.concatenate([tokens, cotangent], axis=1)
    dispatched = jnp.dot(
        placed.astype(jnp.bfloat16), stacked, preferred_element_type=jnp.float32
    ).astype(jnp.bfloat16)
    expert_in, expert_cot = (
        lax.all_gather(dispatched[:, :local_cols], "hid", axis=1, tiled=True),
        lax.all_gather(dispatched[:, local_cols:], "hid", axis=1, tiled=True),
    )
    router_cols = lax.dynamic_slice_in_dim(
        router, lax.axis_index("hid") * local_cols, local_cols, 1
    )
    logits = lax.psum(contract_cols(tokens, router_cols), "hid")
    other = first + second
    labels = jnp.arange(logits.shape[1], dtype=jnp.int32)
    other_logit = jnp.sum(jnp.where(other[:, None] == labels[None, :], logits, 0.0), axis=1)
    gating = jnp.where(routed, jax.nn.sigmoid(logits[:, 0] - other_logit), 0.0)
    slot_gate = jnp.sum(jnp.where(placed, gating[None, :], 0.0), axis=1)
    weights_in = gate_up.reshape(weight_rows, 2 * hidden_local)
    spread_in, spread_cot = (
        lax.all_to_all(expert_in, "tok", split_axis=1, concat_axis=0, tiled=True),
        lax.all_to_all(expert_cot, "tok", split_axis=1, concat_axis=0, tiled=True),
    )
    rows_in = spread_in
    rows_cot = spread_cot
    sums = lax.psum_scatter(
        jnp.concatenate(
            [
                jnp.dot(rows_in, weights_in, preferred_element_type=jnp.float32),
                jnp.dot(rows_cot, w_down, preferred_element_type=jnp.float32),
            ],
            axis=1,
        ),
        "tok",
        scatter_dimension=0,
        tiled=True,
    )
    grads_mid, scaled, score_part = local_grads(
        sums[:, : 2 * hidden_local], sums[:, 2 * hidden_local :], slot_gate
    )
    packed = jnp.concatenate([grads_mid, scaled], axis=1)
    piece = lax.all_gather(packed, "tok", axis=0, tiled=True)
    start = jnp.int32(0)
    grad_sum = jnp.zeros((weight_rows, 3 * hidden_local), jnp.float32)
    for group in range(piece.shape[0] // CAP):
        first_row = start + group * CAP
        rows_in = lax.dynamic_slice_in_dim(spread_in, first_row, CAP, 0)
        rows_cot = lax.dynamic_slice_in_dim(spread_cot, first_row, CAP, 0)
        section = piece[group * CAP : (group + 1) * CAP]
        term = jnp.concatenate(
            [
                contract_rows(rows_in, section[:, : 2 * hidden_local]),
                contract_rows(rows_cot, section[:, 2 * hidden_local :]),
            ],
            axis=1,
        )
        grad_sum = grad_sum + lax.optimization_barrier(term.astype(jnp.bfloat16)).astype(
            jnp.float32
        )
    block = contract_cols(piece[:, : 2 * hidden_local], weights_in)
    expert_back = lax.all_to_all(block, "tok", split_axis=0, concat_axis=1, tiled=True)
    back_cols = lax.psum_scatter(expert_back, "hid", scatter_dimension=1, tiled=True)
    scores = lax.psum(score_part, "hid")
    safe = jnp.minimum(slot_rank, CAP - 1)
    grad_tokens = jnp.where(routed[:, None], jnp.take(back_cols, safe, axis=0), 0.0).astype(
        jnp.bfloat16
    )
    token_score = jnp.where(routed, jnp.take(scores, safe, axis=0), 0.0)
    d_combine = jnp.stack(
        [jnp.where(in_first, token_score, 0.0), jnp.where(in_second, token_score, 0.0)], axis=1
    )
    d_gate_up = grad_sum[:, : 2 * hidden_local].reshape(weight_rows, 2, hidden_local)
    d_down = grad_sum[:, 2 * hidden_local :]
    return (grad_tokens, d_combine, d_gate_up, d_down)


def solution(mesh):
    in_specs = (
        P("tok", "hid"),
        P("tok", "hid"),
        P("tok", None),
        P(),
        P("tok", None, "hid"),
        P("tok", "hid"),
    )
    out_specs = (P("tok", "hid"), P("tok", None), P("tok", None, "hid"), P("tok", "hid"))
    return jax.shard_map(local, mesh=mesh, in_specs=in_specs, out_specs=out_specs, check_vma=False)
```

profile of v0, /device:TPU:0, one launch (start us, length us, event | category | flops | bytes accessed | tf_op | source)
XLA Modules:
  0.0 836.1 jit_solution(18197287051668682821)
XLA Ops:
  7.2 0.0 all-gather.6.cloned.1.call-start
  7.2 0.9 convert_reduce_fusion
  8.1 0.3 reduce-window.9
  8.4 0.1 slice.112
  8.5 0.1 slice_reduce_fusion
  8.7 0.1 add_bitcast_fusion
  8.7 0.6 fusion.24
  9.4 0.1 bitcast_subtract_fusion
  9.5 4.6 fusion.4
  14.1 1.1 fusion.25
  15.2 0.0 all-gather.6.cloned.1.call-update
  15.2 0.0 all-gather.4.cloned.1.call-start
  15.3 0.7 all-gather.4.cloned.1.call-update
  16.0 58.6 %all-gather.6.cloned.1.call-done = bf16[432,6144]{1,0:T(8,128)(2,1)} async-done(((bf16[432,768]{1,0:T(8,128)(2,1)}), bf16[432,6144]{1,0:T(8,128)(2,1)}) %all-gather.6.cloned.1.call-update) | async-done | bytes 5308432 | tf_op jit(solution)/shard_map/all_gather | solution.py:65
  74.6 5.3 copy.41
  80.0 5.2 all-to-all-start.1
  85.2 47.0 %all-gather.4.cloned.1.call-done = bf16[432,6144]{1,0:T(8,128)(2,1)} async-done(((bf16[432,768]{1,0:T(8,128)(2,1)}), bf16[432,6144]{1,0:T(8,128)(2,1)}) %all-gather.4.cloned.1.call-update) | async-done | bytes 5308432 | tf_op jit(solution)/shard_map/all_gather | solution.py:64
  132.1 5.4 copy.42
  137.5 7.7 all-to-all-done.1
  145.2 5.0 all-to-all-start
  150.2 0.6 reduce-scatter.3.cloned.1.call-start
  150.8 8.1 copy.36
  158.9 10.2 %fusion.27 = f32[1728,1024]{1,0:T(8,128)} fusion(bf16[1728,1536]{1,0:T(8,128)(2,1)} %bitcast.5, bf16[1536,1024]{1,0:T(8,128)(2,1)S(1)} %copy-done), kind=kOutput, calls=%fused_computation.80 | convolution fusion | flops 5435817984 | bytes 15532032 | tf_op jit(solution)/shard_map/dot_general | solution.py:87
  169.1 40.3 %all-to-all-done = bf16[432,4,1536]{2,0,1:T(8,128)(2,1)} async-done(((bf16[432,4,1536]{2,0,1:T(8,128)(2,1)}), bf16[432,4,1536]{2,0,1:T(8,128)(2,1)}, u32[]{:S(2)}, u32[]{:S(2)}) %all-to-all-start) | async-done | bytes 5308448 | tf_op jit(solution)/shard_map/all_to_all | solution.py:78
  209.4 15.1 %fusion.26 = f32[1728,2048]{1,0:T(8,128)S(1)} fusion(bf16[1728,1536]{1,0:T(8,128)(2,1)} %bitcast.3, bf16[1536,2048]{1,0:T(8,128)(2,1)} %bitcast.75), kind=kOutput, calls=%fused_computation.79 | convolution fusion | flops 10871635968 | bytes 25755648 | tf_op jit(solution)/shard_map/dot_general | solution.py:86
  224.5 7.4 pad_maximum_fusion
  231.9 0.0 all-gather.8.cloned.1.call-start
  232.0 1.6 copy-done.3
  233.6 1.4 convolution_bitcast_fusion
  235.0 184.7 %reduce-scatter.3.cloned.1.call-done = f32[432,3072]{1,0:T(8,128)} async-done(((f32[1728,3072]{1,0:T(8,128)}), f32[432,3072]{1,0:T(8,128)}) %reduce-scatter.3.cloned.1.call-update) | async-done | bytes 5308432 | tf_op jit(solution)/shard_map/reduce_scatter | solution.py:83
  419.7 3.1 multiply_reduce_fusion
  422.8 29.1 %all-reduce = (f32[1536,8]{0,1:T(8,128)S(1)}, f32[432]{0:T(512)S(1)}) all-reduce(f32[1536,8]{0,1:T(8,128)S(1)} %convolution_bitcast_fusion, f32[432]{0:T(512)S(1)} %multiply_reduce_fusion), channel_id=1, replica_groups=mesh['tok'=4,'hid'=8] {'hid'}, use_global_device_ids=true, to_apply=%region_2.3 | all-reduce | flops 12720 | bytes 101760 | tf_op jit(solution)/shard_map/psum | solution.py:70
  452.0 0.6 select_reduce_fusion
  452.6 3.9 multiply_convert_fusion.2
  456.5 1.7 pad_maximum_fusion.5
  458.1 0.0 all-gather.8.cloned.1.call-update
  458.2 0.0 reduce-scatter.5.cloned.1.call-start
  458.2 11.5 %reshape.153 = bf16[1536,2048,1]{1,0,2:T(8,128)(2,1)} reshape(bf16[1536,2,1024]{2,1,0:T(2,128)(2,1)} %param.10) | data formatting | bytes 12582912 | tf_op jit(solution)/shard_map/reshape | solution.py:76
  469.8 91.8 %all-gather.8.cloned.1.call-done = bf16[1728,3072]{1,0:T(8,128)(2,1)} async-done(((bf16[432,3072]{1,0:T(8,128)(2,1)}), bf16[1728,3072]{1,0:T(8,128)(2,1)}) %all-gather.8.cloned.1.call-update) | async-done | bytes 10616848 | tf_op jit(solution)/shard_map/all_gather | solution.py:99
  561.6 3.1 slice-done.3
  564.7 13.5 %fusion.28 = f32[4,432,1536]{2,1,0:T(8,128)S(1)} fusion(bf16[4,432,2048]{2,1,0:T(8,128)(2,1)S(1)} %bitcast.74, bf16[1536,2048,1]{1,0,2:T(8,128)(2,1)} %reshape.153), kind=kOutput, calls=%fused_computation.81 | convolution fusion | flops 10871635968 | bytes 23986176 | tf_op jit(solution)/shard_map/dot_general | solution.py:21
  578.2 119.8 %all_to_all.54 = f32[4,432,1536]{2,1,0:T(8,128)S(1)} all-to-all(f32[4,432,1536]{2,1,0:T(8,128)S(1)} %fusion.28), channel_id=1, replica_groups=mesh['tok'=4,'hid'=8] {'tok'}, dimensions={0} | all-to-all | bytes 21233664 | tf_op jit(solution)/shard_map/all_to_all | solution.py:118
  698.0 5.3 copy.34
  703.4 9.5 %gather_fusion.1 = f32[1536]{0:T(1024)S(1)} fusion(f32[432]{0:T(512)S(1)} %get-tuple-element.5, s32[2048]{0:T(1024)S(1)} %pad_clamp_fusion), kind=kCustom, calls=%fused_computation.1 | custom fusion | bytes 18432 | tf_op jit(solution)/shard_map/jit(_take)/gather | solution.py:125
  713.0 0.6 pad_maximum_fusion.6
  713.6 3.4 convolution_convert_fusion.4
  717.0 5.5 convolution_convert_fusion
  722.6 0.8 pad_maximum_fusion.4
  723.5 0.8 slice-done.2
  724.2 3.2 convolution_convert_fusion.5
  727.4 5.1 convolution_convert_fusion.1
  732.5 1.1 pad_maximum_fusion.3
  733.6 3.4 convolution_convert_fusion.6
  737.0 8.1 convolution_convert_fusion.2
  745.1 4.7 pad_maximum_fusion.2
  749.8 3.4 convolution_convert_fusion.7
  753.2 8.1 convolution_convert_fusion.3
  761.3 7.8 pad_maximum_fusion.1
  769.1 13.3 %convert_add_fusion = f32[1536,3072]{1,0:T(8,128)} fusion(bf16[1536,3072]{1,0:T(8,128)(2,1)S(1)} %pad_maximum_fusion.4, bf16[1536,3072]{1,0:T(8,128)(2,1)S(1)} %pad_maximum_fusion.3, bf16[1536,3072]{1,0:T(8,128)(2,1)S(1)} %pad_maximum_fusion.2, bf16[1536,3072]{1,0:T(8,128)(2,1)} %pad_maximum_fusion.1), kind=kLoop, calls=%fused_computation.3 | loop fusion | flops 33030144 | bytes 56623104 | tf_op jit(solution)/shard_map/add | solution.py:114
  782.4 11.5 %slice.129 = f32[1536,2048]{1,0:T(8,128)} slice(f32[1536,3072]{1,0:T(8,128)} %convert_add_fusion), slice={[0:1536], [0:2048]} | slice | bytes 25165824 | tf_op jit(solution)/shard_map/slice | solution.py:129
  793.8 6.7 slice.130
  800.5 16.9 %reshape.135 = f32[1536,2,1024]{2,1,0:T(2,128)} reshape(f32[1536,2048]{1,0:T(8,128)} %slice.129) | data formatting | bytes 25165824 | tf_op jit(solution)/shard_map/reshape | solution.py:129
  817.4 8.2 gather_fusion
  825.6 3.5 select_convert_fusion
  (33 shorter events, 0.2 us)
Async XLA Ops:
  7.2 151.7 %copy-start = (bf16[1536,1024]{1,0:T(8,128)(2,1)S(1)}, bf16[1536,1024]{1,0:T(8,128)(2,1)}, u32[]{:S(2)}) copy-start(bf16[1536,1024]{1,0:T(8,128)(2,1)} %param.11) | copy-start | bytes 9437188
  7.2 67.4 %all-gather.6.cloned.1.call-start = ((), (), s32[]{:S(2)}) async-start(), calls=%async_computation.6 | async-start | bytes 5971968 | tf_op jit(solution)/shard_map/all_gather | solution.py:65
  9.4 442.6 %copy-start.4 = (pred[1536]{0:T(1024)(128)(4,1)}, pred[1536]{0:T(1024)(128)(4,1)S(1)}, u32[]{:S(2)}) copy-start(pred[1536]{0:T(1024)(128)(4,1)S(1)} %get-tuple-element.18) | copy-start | bytes 4612
  15.2 116.9 %all-gather.4.cloned.1.call-start = ((), (), s32[]{:S(2)}) async-start(), calls=%async_computation.5 | async-start | bytes 5971968 | tf_op jit(solution)/shard_map/all_gather | solution.py:64
  80.0 65.2 %all-to-all-start.1 = ((bf16[432,4,1536]{2,0,1:T(8,128)(2,1)}), bf16[432,4,1536]{2,0,1:T(8,128)(2,1)}, u32[]{:S(2)}, u32[]{:S(2)}) async-start(bf16[432,4,1536]{2,0,1:T(8,128)(2,1)} %bitcast.71), calls=%async_computation.1 | async-start | bytes 10616832 | tf_op jit(solution)/shard_map/all_to_all | solution.py:79
  145.2 64.2 %all-to-all-start = ((bf16[432,4,1536]{2,0,1:T(8,128)(2,1)}), bf16[432,4,1536]{2,0,1:T(8,128)(2,1)}, u32[]{:S(2)}, u32[]{:S(2)}) async-start(bf16[432,4,1536]{2,0,1:T(8,128)(2,1)} %bitcast.70), calls=%async_computation | async-start | bytes 10616832 | tf_op jit(solution)/shard_map/all_to_all | solution.py:78
  150.2 269.5 %reduce-scatter.3.cloned.1.call-start = ((), (), s32[]{:S(2)}) async-start(), calls=%async_computation.7 | async-start | bytes 26542080 | tf_op jit(solution)/shard_map/reduce_scatter | solution.py:83
  209.4 15.1 %copy-start.2 = (f32[1728,1024]{1,0:T(8,128)S(1)}, f32[1728,1024]{1,0:T(8,128)}, u32[]{:S(2)}) copy-start(f32[1728,1024]{1,0:T(8,128)} %fusion.27) | copy-start | bytes 21233668
  231.9 1.7 copy-start.3
  231.9 329.7 %all-gather.8.cloned.1.call-start = ((), (), s32[]{:S(2)}) async-start(), calls=%async_computation.8 | async-start | bytes 13271040 | tf_op jit(solution)/shard_map/all_gather | solution.py:99
  458.2 359.3 %reduce-scatter.5.cloned.1.call-start = ((), (), s32[]{:S(2)}) async-start(), calls=%async_computation.9 | async-start | bytes 11943936 | tf_op jit(solution)/shard_map/reduce_scatter | solution.py:119
  561.6 3.1 slice-start.3
  703.4 9.5 %copy-start.6 = (s32[1536,2]{0,1:T(2,128)S(1)}, s32[1536,2]{0,1:T(2,128)}, u32[]{:S(2)}) copy-start(s32[1536,2]{0,1:T(2,128)} %param.8) | copy-start | bytes 36868
  717.0 6.4 slice-start
  717.0 6.4 slice-start.1
  722.6 1.6 slice-start.2
  817.4 8.2 copy-start.5
  817.4 8.2 copy-start.7
  817.4 11.7 %copy-start.1 = (bf16[1536,1024]{1,0:T(8,128)(2,1)S(1)}, bf16[1536,1024]{1,0:T(8,128)(2,1)}, u32[]{:S(2)}) copy-start(bf16[1536,1024]{1,0:T(8,128)(2,1)} %param.11) | copy-start | bytes 9437188
Sparse Core Ops, SparseCore 0:
  15.3 59.2 all-gather.5
  76.8 55.2 all-gather.3
  232.0 187.5 reduce-scatter.2
  458.3 103.2 all-gather.7
  703.5 110.0 reduce-scatter.4
where the time goes:
time: 841 us; the launch traced here: 836 us
  waiting for transfers between devices  431 us (51%)
  blocking collectives  149 us (18%)
  local copies, waits for them, and re-layouts  95.3 us (11%)
  matrix products  84.9 us (10%)
  other arithmetic  50.7 us (6%)
  between operations  14.6 us (2%)
  starting transfers between devices  11 us (1%)
    reduce_scatter x1, waiting for transfers between devices, local(): lax.psum_scatter(jnp.concatenate([jnp.dot(rows_in, weights_in, preferred_...  185 us
    all_to_all x1, blocking collectives, local(): lax.all_to_all(block, 'tok', split_axis=0, concat_axis=1, tiled=True)  120 us
    all_gather x1, waiting for transfers between devices, local(): piece = lax.all_gather(packed, 'tok', axis=0, tiled=True)  91.8 us
    all_gather x1, waiting for transfers between devices, local(): lax.all_gather(dispatched[:, local_cols:], 'hid', axis=1, tiled=True)  58.6 us
    all_gather x1, waiting for transfers between devices, local(): lax.all_gather(dispatched[:, :local_cols], 'hid', axis=1, tiled=True)  47 us
    all_to_all x1, waiting for transfers between devices, local(): lax.all_to_all(expert_in, 'tok', split_axis=1, concat_axis=0, tiled=True)  40.3 us
    dot_general x8, matrix products, contract_rows(): lax.dot_general(left, right, (((0,), (0,)), ((), ())), preferred_element_...  40.1 us
    psum x1, blocking collectives, local(): logits = lax.psum(contract_cols(tokens, router_cols), 'hid')  29.1 us
  transfers between devices with their start and end apart: 7, of which 6 were waited for; matrix products, arithmetic and copies ran while one was open for 19% of the time, Pallas kernels for 0%

commit v1 on v0

--- a/solution.py
+++ b/solution.py
@@ -96,7 +96,13 @@
         sums[:, : 2 * hidden_local], sums[:, 2 * hidden_local :], slot_gate
     )
     packed = jnp.concatenate([grads_mid, scaled], axis=1)
-    piece = lax.all_gather(packed, "tok", axis=0, tiled=True)
+    devices = lax.axis_size("tok")
+    moving, tiles = (packed, [packed])
+    for _ in range(devices - 1):
+        moving = lax.ppermute(moving, "tok", [(i, (i + 1) % devices) for i in range(devices)])
+        tiles.insert(0, moving)
+    merged = jnp.concatenate(tiles, axis=0)
+    piece = jnp.roll(merged, (lax.axis_index("tok") + 1) * packed.shape[0], axis=0)
     start = jnp.int32(0)
     grad_sum = jnp.zeros((weight_rows, 3 * hidden_local), jnp.float32)
     for group in range(piece.shape[0] // CAP):

time: 841 us -> 937 us (1.11)
  waiting for transfers between devices: 431 us -> 503 us
  local copies, waits for them, and re-layouts: 95.3 us -> 115 us
    ppermute x0 -> x3, waiting for transfers between devices: none -> 156 us  [local(): lax.ppermute(moving, 'tok', [(i, (i + 1) % devices) for i in range(device...]
    all_gather x1 -> x0, waiting for transfers between devices: 91.8 us -> none  [local(): piece = lax.all_gather(packed, 'tok', axis=0, tiled=True)]
    unnamed x23 -> x33, local copies, waits for them, and re-layouts: 10.5 us -> 29 us
  transfers between devices with their start and end apart: 7 -> 9, of which waited for: 6 -> 9; matrix products, arithmetic and copies ran while one was open for 19% -> 17% of each run, Pallas kernels for 0% -> 0%
where the time goes in v1:
time: 937 us; the launch traced here: 928 us
  waiting for transfers between devices  503 us (54%)
  blocking collectives  143 us (15%)
  local copies, waits for them, and re-layouts  115 us (12%)
  matrix products  85.9 us (9%)
  other arithmetic  53 us (6%)
  between operations  14.3 us (2%)
  starting transfers between devices  13.7 us (1%)
    reduce_scatter x1, waiting for transfers between devices, local(): lax.psum_scatter(jnp.concatenate([jnp.dot(rows_in, weights_in, preferred_...  185 us
    ppermute x3, waiting for transfers between devices, local(): lax.ppermute(moving, 'tok', [(i, (i + 1) % devices) for i in range(device...  156 us
    all_to_all x1, blocking collectives, local(): lax.all_to_all(block, 'tok', split_axis=0, concat_axis=1, tiled=True)  114 us
    all_gather x1, waiting for transfers between devices, local(): lax.all_gather(dispatched[:, local_cols:], 'hid', axis=1, tiled=True)  58.6 us
    all_gather x1, waiting for transfers between devices, local(): lax.all_gather(dispatched[:, :local_cols], 'hid', axis=1, tiled=True)  47 us
    dot_general x8, matrix products, contract_rows(): lax.dot_general(left, right, (((0,), (0,)), ((), ())), preferred_element_...  41.2 us
    all_to_all x1, waiting for transfers between devices, local(): lax.all_to_all(expert_in, 'tok', split_axis=1, concat_axis=0, tiled=True)  40.7 us
    psum x1, blocking collectives, local(): logits = lax.psum(contract_cols(tokens, router_cols), 'hid')  29.1 us
  transfers between devices with their start and end apart: 9, of which 9 were waited for; matrix products, arithmetic and copies ran while one was open for 17% of the time, Pallas kernels for 0%

profile of v1, /device:TPU:0, one launch (start us, length us, event | category | flops | bytes accessed | tf_op | source)
XLA Modules:
  0.0 928.3 jit_solution(11078693574408264709)
XLA Ops:
  7.2 0.9 convert_reduce_fusion
  8.7 1.2 fusion.28
  10.0 4.6 fusion.4
  14.7 1.1 fusion.29
  15.9 0.7 all-gather.3.cloned.1.call-update
  16.6 58.6 %all-gather.5.cloned.1.call-done = bf16[432,6144]{1,0:T(8,128)(2,1)} async-done(((bf16[432,768]{1,0:T(8,128)(2,1)}), bf16[432,6144]{1,0:T(8,128)(2,1)}) %all-gather.5.cloned.1.call-update) | async-done | bytes 5308432 | tf_op jit(solution)/shard_map/all_gather | solution.py:65
  75.2 5.3 copy.41
  80.6 5.1 all-to-all-start.1
  85.7 47.0 %all-gather.3.cloned.1.call-done = bf16[432,6144]{1,0:T(8,128)(2,1)} async-done(((bf16[432,768]{1,0:T(8,128)(2,1)}), bf16[432,6144]{1,0:T(8,128)(2,1)}) %all-gather.3.cloned.1.call-update) | async-done | bytes 5308432 | tf_op jit(solution)/shard_map/all_gather | solution.py:64
  132.7 5.4 copy.42
  138.1 7.7 all-to-all-done.1
  145.7 5.1 all-to-all-start
  151.1 8.1 copy.36
  159.2 10.2 %fusion.31 = f32[1728,1024]{1,0:T(8,128)} fusion(bf16[1728,1536]{1,0:T(8,128)(2,1)} %bitcast.5, bf16[1536,1024]{1,0:T(8,128)(2,1)S(1)} %copy-done), kind=kOutput, calls=%fused_computation.93 | convolution fusion | flops 5435817984 | bytes 15532032 | tf_op jit(solution)/shard_map/dot_general | solution.py:87
  169.3 40.7 %all-to-all-done = bf16[432,4,1536]{2,0,1:T(8,128)(2,1)} async-done(((bf16[432,4,1536]{2,0,1:T(8,128)(2,1)}), bf16[432,4,1536]{2,0,1:T(8,128)(2,1)}, u32[]{:S(2)}, u32[]{:S(2)}) %all-to-all-start) | async-done | bytes 5308448 | tf_op jit(solution)/shard_map/all_to_all | solution.py:78
  210.0 15.1 %fusion.30 = f32[1728,2048]{1,0:T(8,128)S(1)} fusion(bf16[1728,1536]{1,0:T(8,128)(2,1)} %bitcast.3, bf16[1536,2048]{1,0:T(8,128)(2,1)} %bitcast.73), kind=kOutput, calls=%fused_computation.92 | convolution fusion | flops 10871635968 | bytes 25755648 | tf_op jit(solution)/shard_map/dot_general | solution.py:86
  225.1 7.5 pad_maximum_fusion
  232.7 1.6 copy-done.5
  234.3 1.4 convolution_bitcast_fusion
  235.7 184.7 %reduce-scatter.3.cloned.1.call-done = f32[432,3072]{1,0:T(8,128)} async-done(((f32[1728,3072]{1,0:T(8,128)}), f32[432,3072]{1,0:T(8,128)}) %reduce-scatter.3.cloned.1.call-update) | async-done | bytes 5308432 | tf_op jit(solution)/shard_map/reduce_scatter | solution.py:83
  420.4 3.1 multiply_reduce_fusion
  423.5 29.1 %all-reduce = (f32[1536,8]{0,1:T(8,128)S(1)}, f32[432]{0:T(512)S(1)}) all-reduce(f32[1536,8]{0,1:T(8,128)S(1)} %convolution_bitcast_fusion, f32[432]{0:T(512)S(1)} %multiply_reduce_fusion), channel_id=1, replica_groups=mesh['tok'=4,'hid'=8] {'hid'}, use_global_device_ids=true, to_apply=%region_2.3 | all-reduce | flops 12720 | bytes 101760 | tf_op jit(solution)/shard_map/psum | solution.py:70
  453.3 3.9 multiply_convert_fusion.2
  457.4 1.5 collective-permute-start
  458.9 55.3 %collective-permute-done = bf16[432,3072]{1,0:T(8,128)(2,1)S(1)} collective-permute-done((bf16[432,3072]{1,0:T(8,128)(2,1)S(1)}, bf16[432,3072]{1,0:T(8,128)(2,1)S(1)}, u32[]{:S(2)}, u32[]{:S(2)}) %collective-permute-start) | collective-permute-done | bytes 2654240 | tf_op jit(solution)/shard_map/ppermute | solution.py:102
  514.3 1.5 copy-done.2
  515.8 0.9 collective-permute-start.1
  516.7 56.6 %collective-permute-done.1 = bf16[432,3072]{1,0:T(8,128)(2,1)} collective-permute-done((bf16[432,3072]{1,0:T(8,128)(2,1)S(1)}, bf16[432,3072]{1,0:T(8,128)(2,1)}, u32[]{:S(2)}, u32[]{:S(2)}) %collective-permute-start.1) | collective-permute-done | bytes 2654240 | tf_op jit(solution)/shard_map/ppermute | solution.py:102
  573.3 0.6 collective-permute-start.2
  573.9 11.1 %reshape.153 = bf16[1536,2048,1]{1,0,2:T(8,128)(2,1)} reshape(bf16[1536,2,1024]{2,1,0:T(2,128)(2,1)} %param.10) | data formatting | bytes 12582912 | tf_op jit(solution)/shard_map/reshape | solution.py:76
  585.0 43.7 %collective-permute-done.2 = bf16[432,3072]{1,0:T(8,128)(2,1)} collective-permute-done((bf16[432,3072]{1,0:T(8,128)(2,1)}, bf16[432,3072]{1,0:T(8,128)(2,1)}, u32[]{:S(2)}, u32[]{:S(2)}) %collective-permute-start.2) | collective-permute-done | bytes 2654240 | tf_op jit(solution)/shard_map/ppermute | solution.py:102
  628.7 3.5 constant_dynamic-update-slice_fusion.7
  632.2 3.4 constant_dynamic-update-slice_fusion.6
  635.6 1.7 constant_dynamic-update-slice_fusion.5
  637.3 1.7 constant_dynamic-update-slice_fusion.4
  638.9 3.4 constant_dynamic-update-slice_fusion.3
  642.4 3.5 constant_dynamic-update-slice_fusion.2
  645.8 1.6 constant_dynamic-update-slice_fusion.1
  647.5 1.7 constant_dynamic-update-slice_fusion
  649.2 5.2 constant_dynamic-slice_fusion
  654.4 13.5 %fusion.32 = f32[4,432,1536]{2,1,0:T(8,128)S(1)} fusion(bf16[4,432,2048]{2,1,0:T(8,128)(2,1)S(1)} %bitcast.72, bf16[1536,2048,1]{1,0,2:T(8,128)(2,1)} %reshape.153), kind=kOutput, calls=%fused_computation.94 | convolution fusion | flops 10871635968 | bytes 23986176 | tf_op jit(solution)/shard_map/dot_general | solution.py:21
  667.9 114.2 %all_to_all.54 = f32[4,432,1536]{2,1,0:T(8,128)S(1)} all-to-all(f32[4,432,1536]{2,1,0:T(8,128)S(1)} %fusion.32), channel_id=1, replica_groups=mesh['tok'=4,'hid'=8] {'tok'}, dimensions={0} | all-to-all | bytes 21233664 | tf_op jit(solution)/shard_map/all_to_all | solution.py:124
  782.1 5.4 copy.34
  787.5 0.6 copy-done.6
  788.2 9.5 %gather_fusion.1 = f32[1536]{0:T(1024)S(1)} fusion(f32[432]{0:T(512)S(1)} %get-tuple-element.5, s32[2048]{0:T(1024)S(1)} %pad_clamp_fusion), kind=kCustom, calls=%fused_computation.1 | custom fusion | bytes 18432 | tf_op jit(solution)/shard_map/jit(_take)/gather | solution.py:131
  798.4 3.5 convolution_convert_fusion.4
  801.9 5.4 convolution_convert_fusion
  807.3 1.0 pad_maximum_fusion.4
  808.3 3.5 convolution_convert_fusion.5
  811.8 5.4 convolution_convert_fusion.1
  817.2 0.8 pad_maximum_fusion.3
  818.0 3.5 convolution_convert_fusion.6
  821.6 8.1 convolution_convert_fusion.2
  829.7 4.9 pad_maximum_fusion.2
  834.6 3.6 convolution_convert_fusion.7
  838.2 8.1 convolution_convert_fusion.3
  846.4 7.8 pad_maximum_fusion.1
  854.1 13.0 %convert_add_fusion = f32[1536,3072]{1,0:T(8,128)} fusion(bf16[1536,3072]{1,0:T(8,128)(2,1)S(1)} %pad_maximum_fusion.4, bf16[1536,3072]{1,0:T(8,128)(2,1)S(1)} %pad_maximum_fusion.3, bf16[1536,3072]{1,0:T(8,128)(2,1)S(1)} %pad_maximum_fusion.2, bf16[1536,3072]{1,0:T(8,128)(2,1)} %pad_maximum_fusion.1), kind=kLoop, calls=%fused_computation.3 | loop fusion | flops 33030144 | bytes 56623104 | tf_op jit(solution)/shard_map/add | solution.py:120
  867.1 11.5 %slice.120 = f32[1536,2048]{1,0:T(8,128)} slice(f32[1536,3072]{1,0:T(8,128)} %convert_add_fusion), slice={[0:1536], [0:2048]} | slice | bytes 25165824 | tf_op jit(solution)/shard_map/slice | solution.py:135
  878.6 6.6 slice.121
  885.2 16.9 %reshape.135 = f32[1536,2,1024]{2,1,0:T(2,128)} reshape(f32[1536,2048]{1,0:T(8,128)} %slice.120) | data formatting | bytes 25165824 | tf_op jit(solution)/shard_map/reshape | solution.py:135
  902.1 7.8 reduce-scatter.5.cloned.1.call-done
  909.9 8.2 gather_fusion
  918.0 3.5 select_convert_fusion
  (46 shorter events, 2.6 us)
Async XLA Ops:
  7.2 152.0 %copy-start = (bf16[1536,1024]{1,0:T(8,128)(2,1)S(1)}, bf16[1536,1024]{1,0:T(8,128)(2,1)}, u32[]{:S(2)}) copy-start(bf16[1536,1024]{1,0:T(8,128)(2,1)} %param.11) | copy-start | bytes 9437188
  7.2 68.0 %all-gather.5.cloned.1.call-start = ((), (), s32[]{:S(2)}) async-start(), calls=%async_computation.6 | async-start | bytes 5971968 | tf_op jit(solution)/shard_map/all_gather | solution.py:65
  8.1 6.5 copy-start.7
  10.0 442.8 %copy-start.9 = (pred[1536]{0:T(1024)(128)(4,1)}, pred[1536]{0:T(1024)(128)(4,1)S(1)}, u32[]{:S(2)}) copy-start(pred[1536]{0:T(1024)(128)(4,1)S(1)} %get-tuple-element.18) | copy-start | bytes 4612
  15.8 116.9 %all-gather.3.cloned.1.call-start = ((), (), s32[]{:S(2)}) async-start(), calls=%async_computation.5 | async-start | bytes 5971968 | tf_op jit(solution)/shard_map/all_gather | solution.py:64
  80.6 65.2 %all-to-all-start.1 = ((bf16[432,4,1536]{2,0,1:T(8,128)(2,1)}), bf16[432,4,1536]{2,0,1:T(8,128)(2,1)}, u32[]{:S(2)}, u32[]{:S(2)}) async-start(bf16[432,4,1536]{2,0,1:T(8,128)(2,1)} %bitcast.71), calls=%async_computation.1 | async-start | bytes 10616832 | tf_op jit(solution)/shard_map/all_to_all | solution.py:79
  145.7 64.3 %all-to-all-start = ((bf16[432,4,1536]{2,0,1:T(8,128)(2,1)}), bf16[432,4,1536]{2,0,1:T(8,128)(2,1)}, u32[]{:S(2)}, u32[]{:S(2)}) async-start(bf16[432,4,1536]{2,0,1:T(8,128)(2,1)} %bitcast.70), calls=%async_computation | async-start | bytes 10616832 | tf_op jit(solution)/shard_map/all_to_all | solution.py:78
  150.8 269.6 %reduce-scatter.3.cloned.1.call-start = ((), (), s32[]{:S(2)}) async-start(), calls=%async_computation.7 | async-start | bytes 26542080 | tf_op jit(solution)/shard_map/reduce_scatter | solution.py:83
  210.0 15.1 %copy-start.4 = (f32[1728,1024]{1,0:T(8,128)S(1)}, f32[1728,1024]{1,0:T(8,128)}, u32[]{:S(2)}) copy-start(f32[1728,1024]{1,0:T(8,128)} %fusion.31) | copy-start | bytes 21233668
  232.6 1.7 copy-start.5
  232.7 677.2 %reduce-scatter.5.cloned.1.call-start = ((), (), s32[]{:S(2)}) async-start(), calls=%async_computation.8 | async-start | bytes 11943936 | tf_op jit(solution)/shard_map/reduce_scatter | solution.py:125
  457.4 56.9 %collective-permute-start = (bf16[432,3072]{1,0:T(8,128)(2,1)S(1)}, bf16[432,3072]{1,0:T(8,128)(2,1)S(1)}, u32[]{:S(2)}, u32[]{:S(2)}) collective-permute-start(bf16[432,3072]{1,0:T(8,128)(2,1)S(1)} %pad_maximum_fusion.5), channel_id=1, source_target_pairs={{0,8},{8,16},{16,24},{24,0},{1,9},{9,17},{17,25},{25,1},{2,10},{10... | collective-permute-start | bytes 7962632 | tf_op jit(solution)/shard_map/ppermute | solution.py:102
  514.3 1.5 copy-start.2
  515.8 57.5 %collective-permute-start.1 = (bf16[432,3072]{1,0:T(8,128)(2,1)S(1)}, bf16[432,3072]{1,0:T(8,128)(2,1)}, u32[]{:S(2)}, u32[]{:S(2)}) collective-permute-start(bf16[432,3072]{1,0:T(8,128)(2,1)S(1)} %collective-permute-done), channel_id=1, source_target_pairs={{0,8},{8,16},{16,24},{24,0},{1,9},{9,17},{17,25},{25,1},{2,10},{10... | collective-permute-start | bytes 7962632 | tf_op jit(solution)/shard_map/ppermute | solution.py:102
  573.3 55.4 %collective-permute-start.2 = (bf16[432,3072]{1,0:T(8,128)(2,1)}, bf16[432,3072]{1,0:T(8,128)(2,1)}, u32[]{:S(2)}, u32[]{:S(2)}) collective-permute-start(bf16[432,3072]{1,0:T(8,128)(2,1)} %collective-permute-done.1), channel_id=1, source_target_pairs={{0,8},{8,16},{16,24},{24,0},{1,9},{9,17},{17,25},{25,1},{2,10},{10... | collective-permute-start | bytes 7962632 | tf_op jit(solution)/shard_map/ppermute | solution.py:102
  585.0 50.5 %copy-start.3 = (bf16[432,3072]{1,0:T(8,128)(2,1)S(1)}, bf16[432,3072]{1,0:T(8,128)(2,1)}, u32[]{:S(2)}) copy-start(bf16[432,3072]{1,0:T(8,128)(2,1)} %copy-done.2) | copy-start | bytes 7962628
  787.5 0.7 copy-start.6
  787.5 10.2 %copy-start.8 = (pred[1536,1]{0,1:T(4,128)(4,1)S(1)}, pred[1536,1]{0,1:T(4,128)(4,1)}, u32[]{:S(2)}) copy-start(pred[1536,1]{0,1:T(4,128)(4,1)} %copy-done.7) | copy-start | bytes 4612
  787.5 10.2 %copy-start.11 = (s32[1536,2]{0,1:T(2,128)S(1)}, s32[1536,2]{0,1:T(2,128)}, u32[]{:S(2)}) copy-start(s32[1536,2]{0,1:T(2,128)} %param.8) | copy-start | bytes 36868
  902.1 15.9 %copy-start.10 = (pred[1536]{0:T(1024)(128)(4,1)S(1)}, pred[1536]{0:T(1024)(128)(4,1)}, u32[]{:S(2)}) copy-start(pred[1536]{0:T(1024)(128)(4,1)} %copy-done.9) | copy-start | bytes 4612
  902.1 15.9 %copy-start.12 = (pred[1536]{0:T(1024)(128)(4,1)S(1)}, pred[1536]{0:T(1024)(128)(4,1)}, u32[]{:S(2)}) copy-start(pred[1536]{0:T(1024)(128)(4,1)} %get-tuple-element.8) | copy-start | bytes 4612
  909.9 11.7 %copy-start.1 = (bf16[1536,1024]{1,0:T(8,128)(2,1)S(1)}, bf16[1536,1024]{1,0:T(8,128)(2,1)}, u32[]{:S(2)}) copy-start(bf16[1536,1024]{1,0:T(8,128)(2,1)} %param.11) | copy-start | bytes 9437188
Sparse Core Ops, SparseCore 0:
  15.9 59.2 all-gather.4
  77.4 55.2 all-gather.2
  232.8 187.5 reduce-scatter.2
  787.6 122.2 reduce-scatter.4
